TPU v7x, 32 devices: a whole 2x2x4 slice. The times are simulated.
32 devices in a mesh: section: 4 (over z), seq: 8 (over y, x, core).
Axes of the slice: x: 2, y: 2, z: 4, core: 2. Of those that a mesh axis runs over, the one named last changes fastest.
Arguments:
- x_a: bfloat16 [1024, 4096], P('seq'), may hold values from -6 to 6
- x_b: bfloat16 [1024, 4096], P('seq'), may hold values from -6 to 6
- grad_a: bfloat16 [1024, 4096], P('seq'), may hold values from -6 to 6
- grad_b: bfloat16 [1024, 4096], P('seq'), may hold values from -6 to 6
- gains: float32 [4, 2, 4096], P('section'), may hold values from 0.5 to 1.5
- kv_weights: bfloat16 [4, 2, 4096, 1024], P('section'), may hold values from -0.09375 to 0.09375
- doc_lengths: int32 [2, 16], replicated, may hold values from 1 to 128, 1024 in all within a row
Outputs:
- acts: bfloat16 [2, 4, 1024, 4096], P(None, 'section', 'seq')
- in_grads: bfloat16 [2, 4, 1024, 4096], P(None, 'section', 'seq')
- kv_grads: bfloat16 [2, 4, 1024, 1024], P(None, 'section', 'seq')
Inputs may be any that keep to these rules, and one draw needn't show every extreme that they name: `doc_lengths`: each row lists 16 documents that fill the 1024 tokens of its sequence in order; in each row some document is exactly 128 tokens long.
All inputs are finite; a program needn't handle non-finite values.
Results may differ from a plain program's by a relative error of at most 0.024.
Values may be sent and summed in bfloat16 or wider, within the bound.
A program may use at most 320 MiB of HBM per device.

v0:
```python
import math

import jax
import jax.numpy as jnp
from jax import lax
from jax.sharding import PartitionSpec as P

HEADS = 32
HEAD_DIM = 128
KV_HEADS = 4
REACH = 1


epsilon = 1e-05


def passed_along(block, axis, distance):
    devices = range(lax.axis_size(axis))
    route = [(i - distance, i) for i in devices if i - distance in devices]
    return lax.ppermute(block, axis, route)


def normalize(stream, gain_row):
    widened = stream.astype(jnp.float32)
    square_mean = jnp.mean(widened * widened, axis=-1, keepdims=True)
    return (widened * lax.rsqrt(square_mean + epsilon) * gain_row).astype(jnp.bfloat16)


def project_kv(stream, gain_row, weight_mat):
    return jnp.dot(
        normalize(stream, gain_row), weight_mat, preferred_element_type=jnp.float32
    ).astype(jnp.bfloat16)


def doc_index(ends_row, places):
    return jnp.sum((ends_row[None, :] <= places[:, None]).astype(jnp.int32), axis=1)


def mix(stream, gain_row, pair_rows, docs_query, place_query, docs_key, place_key):
    row_count = stream.shape[0]
    widened = stream.astype(jnp.float32)
    normed = normalize(stream, gain_row)
    group_size = HEADS // KV_HEADS
    queries = normed.reshape(row_count, KV_HEADS, group_size, HEAD_DIM)
    key_count = pair_rows.shape[0]
    key_heads = pair_rows[:, : KV_HEADS * HEAD_DIM].reshape(key_count, KV_HEADS, HEAD_DIM)
    value_heads = pair_rows[:, KV_HEADS * HEAD_DIM :].reshape(key_count, KV_HEADS, HEAD_DIM)
    scores = jnp.einsum(
        "tkgd,skd->kgts", queries, key_heads, preferred_element_type=jnp.float32
    ) * (1.0 / math.sqrt(HEAD_DIM))
    allowed = (
        (docs_query[:, None] == docs_key[None, :])
        & (place_key[None, :] <= place_query[:, None])
        & (place_key[None, :] >= 0)
    )
    scores = jnp.where(allowed, scores, -1e30)
    largest = jnp.max(scores, axis=-1, keepdims=True)
    powers = jnp.exp(scores - largest)
    weights = (powers / jnp.sum(powers, axis=-1, keepdims=True)).astype(jnp.bfloat16)
    mixture = jnp.einsum("kgts,skd->tkgd", weights, value_heads, preferred_element_type=jnp.float32)
    return (widened + mixture.reshape(row_count, HEADS * HEAD_DIM)).astype(jnp.bfloat16)


def window_forward(own_pairs):
    earlier = [passed_along(own_pairs, "seq", 1)]
    return jnp.concatenate(earlier + [own_pairs], axis=0)


def window_again(own_pairs):
    earlier = [passed_along(own_pairs, "seq", 1)]
    return jnp.concatenate(earlier + [own_pairs], axis=0)


def return_window(grad_window, row_count):
    total = grad_window[REACH * row_count :]
    piece = grad_window[0:row_count]
    total = total + passed_along(piece, "seq", 0 - REACH)
    return total


def pass_along(message, offset):
    return passed_along(message, "section", offset)


def pass_back(message, offset):
    return passed_along(message, "section", offset)


def per_device(x_a, x_b, grad_a, grad_b, gains, kv_weights, doc_lengths):
    section_count = lax.axis_size("section")
    section_here = lax.axis_index("section")
    shard_here = lax.axis_index("seq")
    row_count = x_a.shape[0]
    own_places = shard_here * row_count + jnp.arange(row_count, dtype=jnp.int32)
    key_places = (
        own_places[0] - REACH * row_count + jnp.arange((REACH + 1) * row_count, dtype=jnp.int32)
    )
    doc_ends = jnp.cumsum(doc_lengths, axis=1)
    query_docs = jnp.stack([doc_index(doc_ends[0], own_places), doc_index(doc_ends[1], own_places)])
    key_docs = jnp.stack([doc_index(doc_ends[0], key_places), doc_index(doc_ends[1], key_places)])
    gain_pair = gains[0]
    weight_pair = kv_weights[0]
    pair_width = weight_pair.shape[-1]

    def layer_setup(slot_index):
        return (
            lax.dynamic_index_in_dim(gain_pair, slot_index, 0, keepdims=False),
            lax.dynamic_index_in_dim(weight_pair, slot_index, 0, keepdims=False),
            lax.dynamic_index_in_dim(query_docs, slot_index, 0, keepdims=False),
            lax.dynamic_index_in_dim(key_docs, slot_index, 0, keepdims=False),
        )

    empty_pairs = jnp.zeros((row_count, pair_width), jnp.bfloat16)
    held_down = x_a
    held_up = x_b
    saved_down = x_a
    saved_up = x_b
    acts_down = jnp.zeros_like(x_a)
    acts_up = jnp.zeros_like(x_a)
    for section_step in range(section_count):
        going_down = section_here == section_step
        going_up = section_here == section_count - 1 - section_step
        active = going_down | going_up
        slot_index = jnp.where(going_down, 0, 1).astype(jnp.int32)
        layer_input = jnp.where(going_down, held_down, held_up)
        gain_row, weight_mat, docs_query, docs_key = layer_setup(slot_index)
        own_pairs = lax.cond(
            active,
            lambda stream_arg: project_kv(stream_arg, gain_row, weight_mat),
            lambda stream_arg: empty_pairs,
            layer_input,
        )
        window = window_forward(own_pairs)
        layer_output = lax.cond(
            active,
            lambda stream_arg, window_arg: mix(
                stream_arg, gain_row, window_arg, docs_query, own_places, docs_key, key_places
            ),
            lambda stream_arg, window_arg: stream_arg,
            layer_input,
            window,
        )
        if section_step + 1 < section_count:
            held_down = pass_along(layer_output, 1)
            held_up = pass_along(layer_output, -1)
        saved_down = jnp.where(going_down, layer_input, saved_down)
        saved_up = jnp.where(going_up, layer_input, saved_up)
        acts_down = jnp.where(going_down, layer_output, acts_down)
        acts_up = jnp.where(going_up, layer_output, acts_up)
    held_down = grad_a
    held_up = grad_b
    ingrad_down = jnp.zeros_like(x_a)
    ingrad_up = jnp.zeros_like(x_a)
    kvgrad_down = empty_pairs
    kvgrad_up = empty_pairs
    for section_step in range(section_count):
        back_down = section_here == section_count - 1 - section_step
        back_up = section_here == section_step
        active = back_down | back_up
        slot_index = jnp.where(back_down, 0, 1).astype(jnp.int32)
        cotangent = jnp.where(back_down, held_down, held_up)
        layer_input = jnp.where(back_down, saved_down, saved_up)
        gain_row, weight_mat, docs_query, docs_key = layer_setup(slot_index)
        own_pairs = lax.cond(
            active,
            lambda stream_arg: project_kv(stream_arg, gain_row, weight_mat),
            lambda stream_arg: empty_pairs,
            layer_input,
        )
        window = window_again(own_pairs)

        def reverse_mix(cotangent_arg, stream_arg, window_arg):
            _, pull_mix = jax.vjp(
                lambda stream_inner, window_inner: mix(
                    stream_inner,
                    gain_row,
                    window_inner,
                    docs_query,
                    own_places,
                    docs_key,
                    key_places,
                ),
                stream_arg,
                window_arg,
            )
            return pull_mix(cotangent_arg)

        def skip_mix(cotangent_arg, stream_arg, window_arg):
            return (jnp.zeros_like(stream_arg), jnp.zeros_like(window_arg))

        grad_stream, grad_window = lax.cond(
            active, reverse_mix, skip_mix, cotangent, layer_input, window
        )
        grad_pairs = return_window(grad_window, row_count)

        def reverse_proj(stream_arg, grad_arg, pairs_arg):
            _, pull_proj = jax.vjp(
                lambda stream_inner: project_kv(stream_inner, gain_row, weight_mat), stream_arg
            )
            return grad_arg + pull_proj(pairs_arg)[0]

        grad_total = lax.cond(
            active,
            reverse_proj,
            lambda stream_arg, grad_arg, pairs_arg: grad_arg,
            layer_input,
            grad_stream,
            grad_pairs,
        )
        ingrad_down = jnp.where(back_down, grad_total, ingrad_down)
        ingrad_up = jnp.where(back_up, grad_total, ingrad_up)
        kvgrad_down = jnp.where(back_down, grad_pairs, kvgrad_down)
        kvgrad_up = jnp.where(back_up, grad_pairs, kvgrad_up)
        if section_step + 1 < section_count:
            held_down = pass_back(grad_total, -1)
            held_up = pass_back(grad_total, 1)
    acts_out = jnp.stack([acts_down, acts_up])[:, None]
    ingrad_out = jnp.stack([ingrad_down, ingrad_up])[:, None]
    kvgrad_out = jnp.stack([kvgrad_down, kvgrad_up])[:, None]
    return (acts_out, ingrad_out, kvgrad_out)


def solution(mesh):
    in_specs = (
        P("seq", None),
        P("seq", None),
        P("seq", None),
        P("seq", None),
        P("section", None, None),
        P("section", None, None, None),
        P(),
    )
    out_specs = (
        P(None, "section", "seq", None),
        P(None, "section", "seq", None),
        P(None, "section", "seq", None),
    )
    return jax.shard_map(
        per_device, mesh=mesh, in_specs=in_specs, out_specs=out_specs, check_vma=False
    )
```

profile of v0, /device:TPU:27, one launch (start us, length us, event | category | flops | bytes accessed | tf_op | source)
XLA Modules:
  0.0 484.7 jit_solution(4887115583704479755)
XLA Ops:
  1.7 21.3 %dynamic-slice_bitcast_fusion = (bf16[4096,1024]{1,0:T(8,128)(2,1)}, bf16[4096,1024]{1,0:T(8,128)(2,1)}, bf16[4096,1024]{1,0:T(8,128)(2,1)S(1)}, bf16[4096,1024]{1,0:T(8,128)(2,1)}) fusion(bf16[1,2,4096,1024]{3,2,1,0:T(8,128)(2,1)} %param.52, s32[]{:T(128)S(6)} %select_n.359, s32[]{:T(128)S(6)} %select_n.355, s32[]{:T(128)S(6)} %select_n.353, s32[]{:T(128)S(6)} %select_n.357), kind=kLoop, calls=%fused_computation.444 | loop fusion | bytes 67108880 | tf_op jit(solution)/shard_map/jit(dynamic_index_in_dim)/squeeze | solution.py:108
  35.1 9.9 %conditional.21 = ((bf16[128,4096]{1,0:T(8,128)(2,1)S(1)})) conditional(s32[]{:T(128)} %convert_element_type.436, (bf16[128,4096]{1,0:T(8,128)(2,1)S(1)}) %tuple.214, (bf16[128,4096]{1,0:T(8,128)(2,1)S(1)}, s32[128]{0:T(128)}, s32[256]{0:T(256)}, s32[256]{0:T(256)S(1)}, s32[128]{0:T(128)S(1)}, /*index=5*/f32[4096]{0:T(1024)S(1)}, ...), branch_computations={%region_8.9_spmd, %region_9.13_spmd} | conditional | flops 548536960 | bytes 24762896 | solution.py:134
  51.3 18.9 %collective-permute-done.1 = bf16[128,4096]{1,0:T(8,128)(2,1)S(1)} collective-permute-done((bf16[128,4096]{1,0:T(8,128)(2,1)S(1)}, bf16[128,4096]{1,0:T(8,128)(2,1)S(1)}, u32[]{:S(2)}, u32[]{:S(2)}) %collective-permute-start.1) | collective-permute-done | bytes 1048608 | tf_op jit(solution)/shard_map/ppermute | solution.py:20
  72.6 5.5 %collective-permute-start.3 = (bf16[128,1024]{0,1:T(8,128)(2,1)S(1)}, bf16[128,1024]{0,1:T(8,128)(2,1)S(1)}, u32[]{:S(2)}, u32[]{:S(2)}) collective-permute-start(bf16[128,1024]{0,1:T(8,128)(2,1)S(1)} %get-tuple-element.690), channel_id=1, source_target_pairs={{0,1},{1,2},{2,3},{3,4},{4,5},{5,6},{6,7},{8,9},{9,10},{10,11},{11... | collective-permute-start | bytes 786440 | tf_op jit(solution)/shard_map/ppermute | solution.py:20
  83.9 21.3 %collective-permute-start.5 = (bf16[128,4096]{1,0:T(8,128)(2,1)}, bf16[128,4096]{1,0:T(8,128)(2,1)S(1)}, u32[]{:S(2)}, u32[]{:S(2)}) collective-permute-start(bf16[128,4096]{1,0:T(8,128)(2,1)} %get-tuple-element.691), channel_id=1, source_target_pairs={{8,0},{16,8},{24,16},{9,1},{17,9},{25,17},{10,2},{18,10},{26,18},{... | collective-permute-start | bytes 3145736 | tf_op jit(solution)/shard_map/ppermute | solution.py:20
  105.2 20.4 %collective-permute-done.4 = bf16[128,4096]{1,0:T(8,128)(2,1)S(1)} collective-permute-done((bf16[128,4096]{1,0:T(8,128)(2,1)}, bf16[128,4096]{1,0:T(8,128)(2,1)S(1)}, u32[]{:S(2)}, u32[]{:S(2)}) %collective-permute-start.4) | collective-permute-done | bytes 1048608 | tf_op jit(solution)/shard_map/ppermute | solution.py:20
  135.1 25.1 %collective-permute-start.8 = (bf16[128,4096]{1,0:T(8,128)(2,1)}, bf16[128,4096]{1,0:T(8,128)(2,1)S(1)}, u32[]{:S(2)}, u32[]{:S(2)}) collective-permute-start(bf16[128,4096]{1,0:T(8,128)(2,1)} %get-tuple-element.694), channel_id=1, source_target_pairs={{8,0},{16,8},{24,16},{9,1},{17,9},{25,17},{10,2},{18,10},{26,18},{... | collective-permute-start | bytes 3145736 | tf_op jit(solution)/shard_map/ppermute | solution.py:20
  160.2 17.0 %collective-permute-done.7 = bf16[128,4096]{1,0:T(8,128)(2,1)S(1)} collective-permute-done((bf16[128,4096]{1,0:T(8,128)(2,1)}, bf16[128,4096]{1,0:T(8,128)(2,1)S(1)}, u32[]{:S(2)}, u32[]{:S(2)}) %collective-permute-start.7) | collective-permute-done | bytes 1048608 | tf_op jit(solution)/shard_map/ppermute | solution.py:20
  181.8 7.0 %conditional.28 = (bf16[128,1024]{0,1:T(8,128)(2,1)S(1)}) conditional(s32[]{:T(128)} %convert_element_type.436, () %tuple.157, (bf16[128,4096]{1,0:T(8,128)(2,1)S(1)}, f32[4096]{0:T(1024)S(1)}, bf16[4096,1024]{1,0:T(8,128)(2,1)}) %tuple.370), branch_computations={%region_46.47_spmd, %region_47.49_spmd} | conditional | flops 1077543040 | bytes 11290632 | solution.py:164
  198.2 29.5 %conditional.29 = (bf16[128,4096]{0,1:T(8,128)(2,1)}, bf16[256,1024]{0,1:T(8,128)(2,1)}) conditional(s32[]{:T(128)} %convert_element_type.436, () %tuple.156, (s32[128]{0:T(128)S(1)}, s32[256]{0:T(256)S(1)}, s32[256]{0:T(256)S(1)}, s32[128]{0:T(128)S(1)}, pred[]{:T(512)}, /*index=5*/bf16[128,4096]{1,0:T(8,128)(2,1)}, bf16[128,4096]{1,0:T(8,128)(2,1)}, ...), branch_computations={%region_49.50_spmd, %region_50.58_spmd} | conditional | flops 1401291776 | bytes 73347912 | solution.py:191
  229.0 6.7 %collective-permute-start.11 = (bf16[128,1024]{1,0:T(8,128)(2,1)S(1)}, bf16[128,1024]{1,0:T(8,128)(2,1)S(1)}, u32[]{:S(2)}, u32[]{:S(2)}) collective-permute-start(bf16[128,1024]{1,0:T(8,128)(2,1)S(1)} %slice.95), channel_id=1, source_target_pairs={{1,0},{2,1},{3,2},{4,3},{5,4},{6,5},{7,6},{9,8},{10,9},{11,10},{12... | collective-permute-start | bytes 786440 | tf_op jit(solution)/shard_map/ppermute | solution.py:20
  238.3 11.1 %conditional.30 = (bf16[128,4096]{1,0:T(8,128)(2,1)}) conditional(s32[]{:T(128)} %convert_element_type.436, (bf16[128,4096]{0,1:T(8,128)(2,1)}) %tuple.232, (bf16[128,1024]{1,0:T(8,128)(2,1)S(1)}, bf16[4096,1024]{1,0:T(8,128)(2,1)}, f32[4096]{0:T(1024)S(1)}, bf16[128,4096]{1,0:T(8,128)(2,1)}, bf16[128,4096]{0,1:T(8,128)(2,1)}) %tuple.372), branch_computations={%region_58.59_spmd, %region_59.62_spmd} | conditional | flops 1081606656 | bytes 27545664 | solution.py:202
  241.0 6.8 %fusion.145 = (f32[128]{0:T(128)S(1)}, f32[128]{0:T(128)S(1)}, f32[128,4096]{1,0:T(8,128)S(1)}) fusion(bf16[128,4096]{1,0:T(8,128)(2,1)} %get-tuple-element.354, f32[4096]{0:T(1024)S(1)} %get-tuple-element.353, bf16[128,1024]{1,0:T(8,128)(2,1)S(1)} %get-tuple-element.351, bf16[4096,1024]{1,0:T(8,128)(2,1)} %get-tuple-element.352), kind=kOutput, calls=%fused_computation.230 | convolution fusion | flops 1077935872 | bytes 11813888 | tf_op jit(solution)/shard_map/cond/branch_1_fun/transpose(jvp())/dot_general | solution.py:30
  262.4 12.4 %collective-permute-done.12 = bf16[128,4096]{0,1:T(8,128)(2,1)S(1)} collective-permute-done((bf16[128,4096]{0,1:T(8,128)(2,1)}, bf16[128,4096]{0,1:T(8,128)(2,1)S(1)}, u32[]{:S(2)}, u32[]{:S(2)}) %collective-permute-start.12) | collective-permute-done | bytes 1048608 | tf_op jit(solution)/shard_map/ppermute | solution.py:20
  294.2 35.6 %collective-permute-start.16 = (bf16[128,4096]{0,1:T(8,128)(2,1)}, bf16[128,4096]{0,1:T(8,128)(2,1)}, u32[]{:S(2)}, u32[]{:S(2)}) collective-permute-start(bf16[128,4096]{0,1:T(8,128)(2,1)} %copy.272), channel_id=1, source_target_pairs={{8,0},{16,8},{24,16},{9,1},{17,9},{25,17},{10,2},{18,10},{26,18},{... | collective-permute-start | bytes 3145736 | tf_op jit(solution)/shard_map/ppermute | solution.py:20
  333.9 7.5 %conditional.26 = (bf16[128,1024]{0,1:T(8,128)(2,1)}) conditional(s32[]{:T(128)} %convert_element_type.436, () %tuple.150, (bf16[128,4096]{1,0:T(8,128)(2,1)S(1)}, f32[4096]{0:T(1024)S(1)}, bf16[4096,1024]{1,0:T(8,128)(2,1)}) %tuple.373), branch_computations={%region_29.30_spmd, %region_30.32_spmd} | conditional | flops 1077543040 | bytes 11290632 | solution.py:127
  334.2 5.4 %convolution_convert_fusion.3 = bf16[128,1024]{1,0:T(8,128)(2,1)} fusion(bf16[4096,1024]{1,0:T(8,128)(2,1)} %get-tuple-element.320, bf16[128,4096]{1,0:T(8,128)(2,1)S(1)} %get-tuple-element.318, f32[4096]{0:T(1024)S(1)} %get-tuple-element.319, f32[128]{0:T(128)S(1)} %add_rsqrt_fusion.6), kind=kOutput, calls=%fused_computation.104 | convolution fusion | flops 1075970048 | bytes 9716224 | tf_op jit(solution)/shard_map/cond/branch_1_fun/dot_general | solution.py:30
  343.4 5.9 %conditional.37 = (bf16[128,1024]{0,1:T(8,128)(2,1)}) conditional(s32[]{:T(128)} %convert_element_type.436, () %tuple.169, (bf16[128,4096]{1,0:T(8,128)(2,1)S(1)}, f32[4096]{0:T(1024)S(1)}, bf16[4096,1024]{1,0:T(8,128)(2,1)}) %tuple.362), branch_computations={%region_37.38_spmd, %region_38.40_spmd} | conditional | flops 1077543040 | bytes 11290632 | solution.py:164
  365.6 16.7 %conditional.27 = ((bf16[128,4096]{1,0:T(8,128)(2,1)})) conditional(s32[]{:T(128)} %convert_element_type.436, (bf16[128,4096]{1,0:T(8,128)(2,1)}) %tuple.229, (bf16[128,4096]{1,0:T(8,128)(2,1)}, s32[128]{0:T(128)S(1)}, s32[256]{0:T(256)S(1)}, s32[256]{0:T(256)S(1)}, s32[128]{0:T(128)S(1)}, /*index=5*/f32[4096]{0:T(1024)S(1)}, ...), branch_computations={%region_32.33_spmd, %region_33.37_spmd} | conditional | flops 548536960 | bytes 24762896 | solution.py:134
  390.2 19.0 %collective-permute-start.20 = (bf16[128,4096]{0,1:T(8,128)(2,1)S(1)}, bf16[128,4096]{0,1:T(8,128)(2,1)S(1)}, u32[]{:S(2)}, u32[]{:S(2)}) collective-permute-start(bf16[128,4096]{0,1:T(8,128)(2,1)S(1)} %copy.281), channel_id=1, source_target_pairs={{8,0},{16,8},{24,16},{9,1},{17,9},{25,17},{10,2},{18,10},{26,18},{... | collective-permute-start | bytes 3145736 | tf_op jit(solution)/shard_map/ppermute | solution.py:20
  414.0 16.4 %collective-permute-done.20 = bf16[128,4096]{0,1:T(8,128)(2,1)S(1)} collective-permute-done((bf16[128,4096]{0,1:T(8,128)(2,1)S(1)}, bf16[128,4096]{0,1:T(8,128)(2,1)S(1)}, u32[]{:S(2)}, u32[]{:S(2)}) %collective-permute-start.20) | collective-permute-done | bytes 1048608 | tf_op jit(solution)/shard_map/ppermute | solution.py:20
  434.6 22.1 %conditional.38 = (bf16[128,4096]{0,1:T(8,128)(2,1)S(1)}, bf16[256,1024]{0,1:T(8,128)(2,1)}) conditional(s32[]{:T(128)} %convert_element_type.436, () %tuple.153, (s32[128]{0:T(128)}, s32[256]{0:T(256)}, s32[256]{0:T(256)S(1)}, s32[128]{0:T(128)S(1)}, pred[]{:T(512)}, /*index=5*/bf16[128,4096]{0,1:T(8,128)(2,1)S(1)}, ...), branch_computations={%region_88.89_spmd, %region_89.97_spmd} | conditional | flops 1401291776 | bytes 69153608 | solution.py:191
  469.9 9.8 %conditional.39 = (bf16[128,4096]{1,0:T(8,128)(2,1)}) conditional(s32[]{:T(128)} %convert_element_type.436, (bf16[128,4096]{0,1:T(8,128)(2,1)S(1)}) %tuple.241, (bf16[128,1024]{1,0:T(8,128)(2,1)}, bf16[4096,1024]{1,0:T(8,128)(2,1)}, f32[4096]{0:T(1024)S(1)}, bf16[128,4096]{1,0:T(8,128)(2,1)S(1)}, bf16[128,4096]{0,1:T(8,128)(2,1)S(1)}) %tuple.364), branch_computations={%region_97.98_spmd, %region_98.101_spmd} | conditional | flops 1081606656 | bytes 23351332 | solution.py:202
  471.4 6.5 %fusion.247 = (f32[128]{0:T(128)S(1)}, f32[128]{0:T(128)S(1)}, f32[128,4096]{1,0:T(8,128)S(1)}) fusion(bf16[128,4096]{1,0:T(8,128)(2,1)S(1)} %get-tuple-element.399, f32[4096]{0:T(1024)S(1)} %get-tuple-element.398, bf16[128,1024]{1,0:T(8,128)(2,1)} %get-tuple-element.396, bf16[4096,1024]{1,0:T(8,128)(2,1)} %get-tuple-element.397), kind=kOutput, calls=%fused_computation.437 | convolution fusion | flops 1077935872 | bytes 11813888 | tf_op jit(solution)/shard_map/cond/branch_1_fun/transpose(jvp())/dot_general | solution.py:30
  (246 shorter events, 256.3 us)
Async XLA Ops:
  28.1 7.0 %collective-permute-start = (bf16[128,1024]{0,1:T(8,128)(2,1)S(1)}, bf16[128,1024]{0,1:T(8,128)(2,1)S(1)}, u32[]{:S(2)}, u32[]{:S(2)}) collective-permute-start(bf16[128,1024]{0,1:T(8,128)(2,1)S(1)} %get-tuple-element.687), channel_id=1, source_target_pairs={{0,1},{1,2},{2,3},{3,4},{4,5},{5,6},{6,7},{8,9},{9,10},{10,11},{11... | collective-permute-start | bytes 786440 | tf_op jit(solution)/shard_map/ppermute | solution.py:20
  45.0 25.2 %collective-permute-start.1 = (bf16[128,4096]{1,0:T(8,128)(2,1)S(1)}, bf16[128,4096]{1,0:T(8,128)(2,1)S(1)}, u32[]{:S(2)}, u32[]{:S(2)}) collective-permute-start(bf16[128,4096]{1,0:T(8,128)(2,1)S(1)} %get-tuple-element.688), channel_id=1, source_target_pairs={{0,8},{8,16},{16,24},{1,9},{9,17},{17,25},{2,10},{10,18},{18,26},{... | collective-permute-start | bytes 3145736 | tf_op jit(solution)/shard_map/ppermute | solution.py:20
  46.3 24.8 %collective-permute-start.2 = (bf16[128,4096]{1,0:T(8,128)(2,1)S(1)}, bf16[128,4096]{1,0:T(8,128)(2,1)}, u32[]{:S(2)}, u32[]{:S(2)}) collective-permute-start(bf16[128,4096]{1,0:T(8,128)(2,1)S(1)} %get-tuple-element.688), channel_id=1, source_target_pairs={{8,0},{16,8},{24,16},{9,1},{17,9},{25,17},{10,2},{18,10},{26,18},{... | collective-permute-start | bytes 3145736 | tf_op jit(solution)/shard_map/ppermute | solution.py:20
  72.6 8.8 %collective-permute-start.3 = (bf16[128,1024]{0,1:T(8,128)(2,1)S(1)}, bf16[128,1024]{0,1:T(8,128)(2,1)S(1)}, u32[]{:S(2)}, u32[]{:S(2)}) collective-permute-start(bf16[128,1024]{0,1:T(8,128)(2,1)S(1)} %get-tuple-element.690), channel_id=1, source_target_pairs={{0,1},{1,2},{2,3},{3,4},{4,5},{5,6},{6,7},{8,9},{9,10},{10,11},{11... | collective-permute-start | bytes 786440 | tf_op jit(solution)/shard_map/ppermute | solution.py:20
  82.6 43.0 %collective-permute-start.4 = (bf16[128,4096]{1,0:T(8,128)(2,1)}, bf16[128,4096]{1,0:T(8,128)(2,1)S(1)}, u32[]{:S(2)}, u32[]{:S(2)}) collective-permute-start(bf16[128,4096]{1,0:T(8,128)(2,1)} %get-tuple-element.691), channel_id=1, source_target_pairs={{0,8},{8,16},{16,24},{1,9},{9,17},{17,25},{2,10},{10,18},{18,26},{... | collective-permute-start | bytes 3145736 | tf_op jit(solution)/shard_map/ppermute | solution.py:20
  83.9 42.7 %collective-permute-start.5 = (bf16[128,4096]{1,0:T(8,128)(2,1)}, bf16[128,4096]{1,0:T(8,128)(2,1)S(1)}, u32[]{:S(2)}, u32[]{:S(2)}) collective-permute-start(bf16[128,4096]{1,0:T(8,128)(2,1)} %get-tuple-element.691), channel_id=1, source_target_pairs={{8,0},{16,8},{24,16},{9,1},{17,9},{25,17},{10,2},{18,10},{26,18},{... | collective-permute-start | bytes 3145736 | tf_op jit(solution)/shard_map/ppermute | solution.py:20
  126.8 5.2 %collective-permute-start.6 = (bf16[128,1024]{0,1:T(8,128)(2,1)S(1)}, bf16[128,1024]{0,1:T(8,128)(2,1)S(1)}, u32[]{:S(2)}, u32[]{:S(2)}) collective-permute-start(bf16[128,1024]{0,1:T(8,128)(2,1)S(1)} %get-tuple-element.693), channel_id=1, source_target_pairs={{0,1},{1,2},{2,3},{3,4},{4,5},{5,6},{6,7},{8,9},{9,10},{10,11},{11... | collective-permute-start | bytes 786440 | tf_op jit(solution)/shard_map/ppermute | solution.py:20
  133.8 43.5 %collective-permute-start.7 = (bf16[128,4096]{1,0:T(8,128)(2,1)}, bf16[128,4096]{1,0:T(8,128)(2,1)S(1)}, u32[]{:S(2)}, u32[]{:S(2)}) collective-permute-start(bf16[128,4096]{1,0:T(8,128)(2,1)} %get-tuple-element.694), channel_id=1, source_target_pairs={{0,8},{8,16},{16,24},{1,9},{9,17},{17,25},{2,10},{10,18},{18,26},{... | collective-permute-start | bytes 3145736 | tf_op jit(solution)/shard_map/ppermute | solution.py:20
  135.1 43.2 %collective-permute-start.8 = (bf16[128,4096]{1,0:T(8,128)(2,1)}, bf16[128,4096]{1,0:T(8,128)(2,1)S(1)}, u32[]{:S(2)}, u32[]{:S(2)}) collective-permute-start(bf16[128,4096]{1,0:T(8,128)(2,1)} %get-tuple-element.694), channel_id=1, source_target_pairs={{8,0},{16,8},{24,16},{9,1},{17,9},{25,17},{10,2},{18,10},{26,18},{... | collective-permute-start | bytes 3145736 | tf_op jit(solution)/shard_map/ppermute | solution.py:20
  188.8 8.5 %collective-permute-start.10 = (bf16[128,1024]{0,1:T(8,128)(2,1)S(1)}, bf16[128,1024]{0,1:T(8,128)(2,1)S(1)}, u32[]{:S(2)}, u32[]{:S(2)}) collective-permute-start(bf16[128,1024]{0,1:T(8,128)(2,1)S(1)} %get-tuple-element.699), channel_id=1, source_target_pairs={{0,1},{1,2},{2,3},{3,4},{4,5},{5,6},{6,7},{8,9},{9,10},{10,11},{11... | collective-permute-start | bytes 786440 | tf_op jit(solution)/shard_map/ppermute | solution.py:20
  229.0 9.3 %collective-permute-start.11 = (bf16[128,1024]{1,0:T(8,128)(2,1)S(1)}, bf16[128,1024]{1,0:T(8,128)(2,1)S(1)}, u32[]{:S(2)}, u32[]{:S(2)}) collective-permute-start(bf16[128,1024]{1,0:T(8,128)(2,1)S(1)} %slice.95), channel_id=1, source_target_pairs={{1,0},{2,1},{3,2},{4,3},{5,4},{6,5},{7,6},{9,8},{10,9},{11,10},{12... | collective-permute-start | bytes 786440 | tf_op jit(solution)/shard_map/ppermute | solution.py:20
  251.6 23.1 %collective-permute-start.12 = (bf16[128,4096]{0,1:T(8,128)(2,1)}, bf16[128,4096]{0,1:T(8,128)(2,1)S(1)}, u32[]{:S(2)}, u32[]{:S(2)}) collective-permute-start(bf16[128,4096]{0,1:T(8,128)(2,1)} %copy.263), channel_id=1, source_target_pairs={{8,0},{16,8},{24,16},{9,1},{17,9},{25,17},{10,2},{18,10},{26,18},{... | collective-permute-start | bytes 3145736 | tf_op jit(solution)/shard_map/ppermute | solution.py:20
  253.0 25.6 %collective-permute-start.13 = (bf16[128,4096]{0,1:T(8,128)(2,1)}, bf16[128,4096]{0,1:T(8,128)(2,1)}, u32[]{:S(2)}, u32[]{:S(2)}) collective-permute-start(bf16[128,4096]{0,1:T(8,128)(2,1)} %copy.263), channel_id=1, source_target_pairs={{0,8},{8,16},{16,24},{1,9},{9,17},{17,25},{2,10},{10,18},{18,26},{... | collective-permute-start | bytes 3145736 | tf_op jit(solution)/shard_map/ppermute | solution.py:20
  255.0 5.5 %collective-permute-start.14 = (bf16[128,1024]{0,1:T(8,128)(2,1)}, bf16[128,1024]{0,1:T(8,128)(2,1)S(1)}, u32[]{:S(2)}, u32[]{:S(2)}) collective-permute-start(bf16[128,1024]{0,1:T(8,128)(2,1)} %get-tuple-element.702), channel_id=1, source_target_pairs={{0,1},{1,2},{2,3},{3,4},{4,5},{5,6},{6,7},{8,9},{9,10},{10,11},{11... | collective-permute-start | bytes 786440 | tf_op jit(solution)/shard_map/ppermute | solution.py:20
  282.1 8.6 %collective-permute-start.15 = (bf16[128,1024]{1,0:T(8,128)(2,1)S(1)}, bf16[128,1024]{1,0:T(8,128)(2,1)S(1)}, u32[]{:S(2)}, u32[]{:S(2)}) collective-permute-start(bf16[128,1024]{1,0:T(8,128)(2,1)S(1)} %slice.97), channel_id=1, source_target_pairs={{1,0},{2,1},{3,2},{4,3},{5,4},{6,5},{7,6},{9,8},{10,9},{11,10},{12... | collective-permute-start | bytes 786440 | tf_op jit(solution)/shard_map/ppermute | solution.py:20
  294.2 58.8 %collective-permute-start.16 = (bf16[128,4096]{0,1:T(8,128)(2,1)}, bf16[128,4096]{0,1:T(8,128)(2,1)}, u32[]{:S(2)}, u32[]{:S(2)}) collective-permute-start(bf16[128,4096]{0,1:T(8,128)(2,1)} %copy.272), channel_id=1, source_target_pairs={{8,0},{16,8},{24,16},{9,1},{17,9},{25,17},{10,2},{18,10},{26,18},{... | collective-permute-start | bytes 3145736 | tf_op jit(solution)/shard_map/ppermute | solution.py:20
  329.8 27.4 %collective-permute-start.17 = (bf16[128,4096]{0,1:T(8,128)(2,1)}, bf16[128,4096]{0,1:T(8,128)(2,1)}, u32[]{:S(2)}, u32[]{:S(2)}) collective-permute-start(bf16[128,4096]{0,1:T(8,128)(2,1)} %copy.272), channel_id=1, source_target_pairs={{0,8},{8,16},{16,24},{1,9},{9,17},{17,25},{2,10},{10,18},{18,26},{... | collective-permute-start | bytes 3145736 | tf_op jit(solution)/shard_map/ppermute | solution.py:20
  331.9 19.3 %collective-permute-start.18 = (bf16[128,1024]{0,1:T(8,128)(2,1)}, bf16[128,1024]{0,1:T(8,128)(2,1)}, u32[]{:S(2)}, u32[]{:S(2)}) collective-permute-start(bf16[128,1024]{0,1:T(8,128)(2,1)} %get-tuple-element.705), channel_id=1, source_target_pairs={{0,1},{1,2},{2,3},{3,4},{4,5},{5,6},{6,7},{8,9},{9,10},{10,11},{11... | collective-permute-start | bytes 786440 | tf_op jit(solution)/shard_map/ppermute | solution.py:20
  341.4 22.2 %collective-permute-start.9 = (bf16[128,1024]{0,1:T(8,128)(2,1)}, bf16[128,1024]{0,1:T(8,128)(2,1)}, u32[]{:S(2)}, u32[]{:S(2)}) collective-permute-start(bf16[128,1024]{0,1:T(8,128)(2,1)} %get-tuple-element.696), channel_id=1, source_target_pairs={{0,1},{1,2},{2,3},{3,4},{4,5},{5,6},{6,7},{8,9},{9,10},{10,11},{11... | collective-permute-start | bytes 786440 | tf_op jit(solution)/shard_map/ppermute | solution.py:20
  349.2 33.1 %collective-permute-start.22 = (bf16[128,1024]{0,1:T(8,128)(2,1)}, bf16[128,1024]{0,1:T(8,128)(2,1)}, u32[]{:S(2)}, u32[]{:S(2)}) collective-permute-start(bf16[128,1024]{0,1:T(8,128)(2,1)} %get-tuple-element.708), channel_id=1, source_target_pairs={{0,1},{1,2},{2,3},{3,4},{4,5},{5,6},{6,7},{8,9},{9,10},{10,11},{11... | collective-permute-start | bytes 786440 | tf_op jit(solution)/shard_map/ppermute | solution.py:20
  361.3 22.8 %collective-permute-start.19 = (bf16[128,1024]{1,0:T(8,128)(2,1)}, bf16[128,1024]{1,0:T(8,128)(2,1)}, u32[]{:S(2)}, u32[]{:S(2)}) collective-permute-start(bf16[128,1024]{1,0:T(8,128)(2,1)} %slice.99), channel_id=1, source_target_pairs={{1,0},{2,1},{3,2},{4,3},{5,4},{6,5},{7,6},{9,8},{10,9},{11,10},{12... | collective-permute-start | bytes 786440 | tf_op jit(solution)/shard_map/ppermute | solution.py:20
  390.2 40.3 %collective-permute-start.20 = (bf16[128,4096]{0,1:T(8,128)(2,1)S(1)}, bf16[128,4096]{0,1:T(8,128)(2,1)S(1)}, u32[]{:S(2)}, u32[]{:S(2)}) collective-permute-start(bf16[128,4096]{0,1:T(8,128)(2,1)S(1)} %copy.281), channel_id=1, source_target_pairs={{8,0},{16,8},{24,16},{9,1},{17,9},{25,17},{10,2},{18,10},{26,18},{... | collective-permute-start | bytes 3145736 | tf_op jit(solution)/shard_map/ppermute | solution.py:20
  409.2 25.4 %collective-permute-start.21 = (bf16[128,4096]{0,1:T(8,128)(2,1)S(1)}, bf16[128,4096]{0,1:T(8,128)(2,1)S(1)}, u32[]{:S(2)}, u32[]{:S(2)}) collective-permute-start(bf16[128,4096]{0,1:T(8,128)(2,1)S(1)} %copy.281), channel_id=1, source_target_pairs={{0,8},{8,16},{16,24},{1,9},{9,17},{17,25},{2,10},{10,18},{18,26},{... | collective-permute-start | bytes 3145736 | tf_op jit(solution)/shard_map/ppermute | solution.py:20
  458.1 8.6 %collective-permute-start.23 = (bf16[128,1024]{1,0:T(8,128)(2,1)S(1)}, bf16[128,1024]{1,0:T(8,128)(2,1)S(1)}, u32[]{:S(2)}, u32[]{:S(2)}) collective-permute-start(bf16[128,1024]{1,0:T(8,128)(2,1)S(1)} %slice.101), channel_id=1, source_target_pairs={{1,0},{2,1},{3,2},{4,3},{5,4},{6,5},{7,6},{9,8},{10,9},{11,10},{12... | collective-permute-start | bytes 786440 | tf_op jit(solution)/shard_map/ppermute | solution.py:20
  (25 other events, 259.4 us)
where the time goes:
time: 493 us; the launch traced here: 485 us
  starting transfers between devices  154 us (31%)
  waiting for transfers between devices  126 us (26%)
  local copies, waits for them, and re-layouts  73.1 us (15%)
  other arithmetic  68.2 us (14%)
  matrix products  59.2 us (12%)
    ppermute x24, starting transfers between devices, passed_along(): return lax.ppermute(block, axis, route)  154 us
    ppermute x24, waiting for transfers between devices, passed_along(): return lax.ppermute(block, axis, route)  126 us
    dot_general x6, matrix products, project_kv(): jnp.dot(normalize(stream, gain_row), weight_mat, preferred_element_type=j...  30.2 us
    squeeze x1, local copies, waits for them, and re-layouts, layer_setup(): lax.dynamic_index_in_dim(weight_pair, slot_index, 0, keepdims=False)  21.3 us
    another operation x12, local copies, waits for them, and re-layouts  17 us
    dot_general x6, matrix products, mix(): jnp.einsum('kgts,skd->tkgd', weights, value_heads, preferred_element_type...  15.5 us
  transfers between devices with their start and end apart: 24, of which 19 were waited for; matrix products, arithmetic and copies ran while one was open for 11% of the time, Pallas kernels for 0%

commit v1 on v0

v1 whole, which is shorter than its diff:
```python
import functools
import math

import jax
import jax.numpy as jnp
from jax import lax
from jax.experimental import pallas as pl
from jax.experimental.pallas import tpu as pltpu
from jax.sharding import PartitionSpec as P

HEADS = 32
HEAD_DIM = 128
KV_HEADS = 4
REACH = 1
GROUP = HEADS // KV_HEADS
SCALE = 1.0 / math.sqrt(HEAD_DIM)

epsilon = 1e-05

F32 = jnp.float32
BF16 = jnp.bfloat16


def passed_along(block, axis, distance):
    devices = range(lax.axis_size(axis))
    route = [(i - distance, i) for i in devices if i - distance in devices]
    return lax.ppermute(block, axis, route)


def dot(a, b, dims):
    return lax.dot_general(a, b, (dims, ((), ())), preferred_element_type=F32)


def project_kernel(slot_ref, h_ref, gain_ref, weight_ref, pairs_ref, normed_ref):
    @pl.when(pl.program_id(0) == 0)
    def _():
        widened = h_ref[...].astype(F32)
        square_mean = jnp.mean(widened * widened, axis=-1, keepdims=True)
        normed_ref[...] = (widened * lax.rsqrt(square_mean + epsilon) * gain_ref[0]).astype(BF16)

    pairs_ref[...] = dot(normed_ref[...], weight_ref[0], ((1,), (0,))).astype(BF16)


def project(slot, stream, gains, weights):
    rows, width = stream.shape
    pair_width = weights.shape[-1]
    tile = pair_width // 4
    return pl.pallas_call(
        project_kernel,
        grid_spec=pltpu.PrefetchScalarGridSpec(
            num_scalar_prefetch=1,
            grid=(pair_width // tile,),
            in_specs=[
                pl.BlockSpec((rows, width), lambda j, s: (0, 0)),
                pl.BlockSpec((1, 1, width), lambda j, s: (s[0], 0, 0)),
                pl.BlockSpec((1, width, tile), lambda j, s: (s[0], 0, j)),
            ],
            out_specs=[
                pl.BlockSpec((rows, tile), lambda j, s: (0, j)),
                pl.BlockSpec((rows, width), lambda j, s: (0, 0)),
            ],
        ),
        out_shape=[
            jax.ShapeDtypeStruct((rows, pair_width), BF16),
            jax.ShapeDtypeStruct((rows, width), BF16),
        ],
        cost_estimate=pl.CostEstimate(
            flops=2 * rows * width * pair_width,
            bytes_accessed=2 * width * pair_width,
            transcendentals=0,
        ),
        name="project",
    )(slot, stream, gains, weights)


def softmax_parts(query, keys, mask):
    scores = dot(query, keys, ((1,), (1,))) * SCALE
    scores = jnp.where(mask, scores, -1e30)
    powers = jnp.exp(scores - jnp.max(scores, axis=-1, keepdims=True))
    return powers * (1.0 / jnp.sum(powers, axis=-1, keepdims=True))


def mix_kernel(h_ref, normed_ref, kp_ref, ko_ref, vp_ref, vo_ref, mask_ref, out_ref):
    keys = jnp.concatenate([kp_ref[...], ko_ref[...]], axis=0)
    values = jnp.concatenate([vp_ref[...], vo_ref[...]], axis=0)
    mask = mask_ref[...] > 0.0
    for head in range(GROUP):
        cols = slice(head * HEAD_DIM, (head + 1) * HEAD_DIM)
        weights = softmax_parts(normed_ref[:, cols], keys, mask).astype(BF16)
        mixture = dot(weights, values, ((1,), (0,)))
        out_ref[:, cols] = (h_ref[:, cols].astype(F32) + mixture).astype(BF16)


def head_specs(rows):
    return [
        pl.BlockSpec((rows, HEAD_DIM), lambda k: (0, k)),
        pl.BlockSpec((rows, HEAD_DIM), lambda k: (0, k)),
        pl.BlockSpec((rows, HEAD_DIM), lambda k: (0, KV_HEADS + k)),
        pl.BlockSpec((rows, HEAD_DIM), lambda k: (0, KV_HEADS + k)),
    ]


def mix(stream, normed, earlier, own, mask):
    rows, width = stream.shape
    block = pl.BlockSpec((rows, GROUP * HEAD_DIM), lambda k: (0, k))
    return pl.pallas_call(
        mix_kernel,
        grid=(KV_HEADS,),
        in_specs=[block, block] + head_specs(rows) + [pl.BlockSpec(mask.shape, lambda k: (0, 0))],
        out_specs=block,
        out_shape=jax.ShapeDtypeStruct((rows, width), BF16),
        cost_estimate=pl.CostEstimate(
            flops=8 * rows * rows * width, bytes_accessed=6 * rows * width, transcendentals=0
        ),
        name="mix",
    )(stream, normed, earlier, own, earlier, own, mask)


def reverse_kernel(
    c_ref, normed_ref, kp_ref, ko_ref, vp_ref, vo_ref, mask_ref,
    dq_ref, dkp_ref, dko_ref, dvp_ref, dvo_ref,
):
    rows = c_ref.shape[0]
    keys = jnp.concatenate([kp_ref[...], ko_ref[...]], axis=0)
    values = jnp.concatenate([vp_ref[...], vo_ref[...]], axis=0)
    mask = mask_ref[...] > 0.0
    weight_list, score_list, query_list, cot_list = [], [], [], []
    for head in range(GROUP):
        cols = slice(head * HEAD_DIM, (head + 1) * HEAD_DIM)
        query = normed_ref[:, cols]
        cot = c_ref[:, cols]
        weights = softmax_parts(query, keys, mask)
        grad_w = dot(cot, values, ((1,), (1,)))
        inner = jnp.sum(grad_w * weights, axis=-1, keepdims=True)
        grad_s = (weights * (grad_w - inner) * SCALE).astype(BF16)
        dq_ref[:, cols] = dot(grad_s, keys, ((1,), (0,))).astype(BF16)
        weight_list.append(weights.astype(BF16))
        score_list.append(grad_s)
        query_list.append(query)
        cot_list.append(cot)
    all_s = jnp.concatenate(score_list, axis=0)
    all_w = jnp.concatenate(weight_list, axis=0)
    all_q = jnp.concatenate(query_list, axis=0)
    all_c = jnp.concatenate(cot_list, axis=0)
    grad_k = dot(all_s, all_q, ((0,), (0,))).astype(BF16)
    grad_v = dot(all_w, all_c, ((0,), (0,))).astype(BF16)
    dkp_ref[...] = grad_k[:rows]
    dko_ref[...] = grad_k[rows:]
    dvp_ref[...] = grad_v[:rows]
    dvo_ref[...] = grad_v[rows:]


def reverse_mix(cotangent, normed, earlier, own, mask):
    rows, width = cotangent.shape
    block = pl.BlockSpec((rows, GROUP * HEAD_DIM), lambda k: (0, k))
    half = pl.BlockSpec((rows, HEAD_DIM), lambda k: (0, k))
    half_shape = jax.ShapeDtypeStruct((rows, KV_HEADS * HEAD_DIM), BF16)
    return pl.pallas_call(
        reverse_kernel,
        grid=(KV_HEADS,),
        in_specs=[block, block] + head_specs(rows) + [pl.BlockSpec(mask.shape, lambda k: (0, 0))],
        out_specs=[block, half, half, half, half],
        out_shape=[jax.ShapeDtypeStruct((rows, width), BF16)] + [half_shape] * 4,
        cost_estimate=pl.CostEstimate(
            flops=20 * rows * rows * width, bytes_accessed=6 * rows * width, transcendentals=0
        ),
        name="reverse_mix",
    )(cotangent, normed, earlier, own, earlier, own, mask)


def reverse_project_kernel(
    steps, slot_ref, c_ref, dq_ref, h_ref, gain_ref, dk_ref, rk_ref, dv_ref, rv_ref, weight_ref,
    total_ref, pairs_ref, grad_scr,
):
    step = pl.program_id(0)
    tile = weight_ref.shape[1]

    @pl.when(step == 0)
    def _():
        half = dk_ref.shape[1]
        pairs_ref[:, :half] = (dk_ref[...].astype(F32) + rk_ref[...].astype(F32)).astype(BF16)
        pairs_ref[:, half:] = (dv_ref[...].astype(F32) + rv_ref[...].astype(F32)).astype(BF16)

    grad_scr[step] = dot(pairs_ref[...], weight_ref[0], ((1,), (1,))).astype(BF16)

    @pl.when(step == steps - 1)
    def _():
        widened = h_ref[...].astype(F32)
        width = widened.shape[1]
        rstd = lax.rsqrt(jnp.mean(widened * widened, axis=-1, keepdims=True) + epsilon)
        inner = jnp.zeros_like(rstd)
        for j in range(steps):
            cols = slice(j * tile, (j + 1) * tile)
            grad_n = (grad_scr[j].astype(F32) + dq_ref[:, cols].astype(F32)) * gain_ref[0, :, cols]
            inner = inner + jnp.sum(grad_n * widened[:, cols], axis=-1, keepdims=True)
        factor = inner * (1.0 / width) * rstd * rstd * rstd
        for j in range(steps):
            cols = slice(j * tile, (j + 1) * tile)
            grad_n = (grad_scr[j].astype(F32) + dq_ref[:, cols].astype(F32)) * gain_ref[0, :, cols]
            grad_h = grad_n * rstd - widened[:, cols] * factor
            total_ref[:, cols] = (c_ref[:, cols].astype(F32) + grad_h).astype(BF16)


def reverse_project(slot, cotangent, grad_q, stream, gains, grads, weights):
    rows, width = stream.shape
    pair_width = weights.shape[-1]
    steps = 4
    tile = width // steps
    full = pl.BlockSpec((rows, width), lambda j, s: (0, 0))
    half = pl.BlockSpec((rows, pair_width // 2), lambda j, s: (0, 0))
    return pl.pallas_call(
        functools.partial(reverse_project_kernel, steps),
        grid_spec=pltpu.PrefetchScalarGridSpec(
            num_scalar_prefetch=1,
            grid=(steps,),
            in_specs=[full, full, full, pl.BlockSpec((1, 1, width), lambda j, s: (s[0], 0, 0))]
            + [half] * 4
            + [pl.BlockSpec((1, tile, pair_width), lambda j, s: (s[0], j, 0))],
            out_specs=[full, pl.BlockSpec((rows, pair_width), lambda j, s: (0, 0))],
            scratch_shapes=[pltpu.VMEM((steps, rows, tile), BF16)],
        ),
        out_shape=[
            jax.ShapeDtypeStruct((rows, width), BF16),
            jax.ShapeDtypeStruct((rows, pair_width), BF16),
        ],
        cost_estimate=pl.CostEstimate(
            flops=2 * rows * width * pair_width,
            bytes_accessed=2 * width * pair_width,
            transcendentals=0,
        ),
        name="reverse_project",
    )(slot, cotangent, grad_q, stream, gains, *grads, weights)


def per_device(x_a, x_b, grad_a, grad_b, gains, kv_weights, doc_lengths):
    count = lax.axis_size("section")
    section = lax.axis_index("section")
    shard = lax.axis_index("seq")
    rows = x_a.shape[0]
    places = shard * rows + jnp.arange(rows, dtype=jnp.int32)
    key_places = (shard - REACH) * rows + jnp.arange((REACH + 1) * rows, dtype=jnp.int32)
    ends = jnp.cumsum(doc_lengths, axis=1)

    def mask_of(direction):
        docs_q = jnp.sum((ends[direction][None, :] <= places[:, None]).astype(jnp.int32), axis=1)
        docs_k = jnp.sum((ends[direction][None, :] <= key_places[:, None]).astype(jnp.int32), axis=1)
        allowed = (
            (docs_q[:, None] == docs_k[None, :])
            & (key_places[None, :] <= places[:, None])
            & (key_places[None, :] >= 0)
        )
        return allowed.astype(F32)

    mask_down, mask_up = mask_of(0), mask_of(1)
    gain_pair = gains[0][:, None, :]
    weight_pair = kv_weights[0]

    saved = {}
    held_down, held_up = x_a, x_b
    for step in range(count):
        down = section == step
        up = section == count - 1 - step
        slot = jnp.where(down, 0, 1).astype(jnp.int32)[None]
        stream = jnp.where(down, held_down, held_up)
        mask = jnp.where(down, mask_down, mask_up)
        own, normed = project(slot, stream, gain_pair, weight_pair)
        earlier = passed_along(own, "seq", REACH)
        output = mix(stream, normed, earlier, own, mask)
        if step + 1 < count:
            held_down = passed_along(output, "section", 1)
            held_up = passed_along(output, "section", -1)
        fresh = (stream, normed, own, earlier, output)
        for name, chosen in (("down", down), ("up", up)):
            before = saved.get(name)
            saved[name] = (
                fresh
                if before is None
                else tuple(jnp.where(chosen, new, old) for new, old in zip(fresh, before))
            )
    acts_out = jnp.stack([saved["down"][4], saved["up"][4]])[:, None]

    held_down, held_up = grad_a, grad_b
    results = {}
    for step in range(count):
        down = section == count - 1 - step
        up = section == step
        slot = jnp.where(down, 0, 1).astype(jnp.int32)[None]
        cotangent = jnp.where(down, held_down, held_up)
        stream, normed, own, earlier = (
            jnp.where(down, a, b) for a, b in zip(saved["down"][:4], saved["up"][:4])
        )
        mask = jnp.where(down, mask_down, mask_up)
        grad_q, dkp, dko, dvp, dvo = reverse_mix(cotangent, normed, earlier, own, mask)
        rk = passed_along(dkp, "seq", 0 - REACH)
        rv = passed_along(dvp, "seq", 0 - REACH)
        total, pairs = reverse_project(
            slot, cotangent, grad_q, stream, gain_pair, (dko, rk, dvo, rv), weight_pair
        )
        if step + 1 < count:
            held_down = passed_along(total, "section", -1)
            held_up = passed_along(total, "section", 1)
        fresh = (total, pairs)
        for name, chosen in (("down", down), ("up", up)):
            before = results.get(name)
            results[name] = (
                fresh
                if before is None
                else tuple(jnp.where(chosen, new, old) for new, old in zip(fresh, before))
            )
    ingrad_out = jnp.stack([results["down"][0], results["up"][0]])[:, None]
    kvgrad_out = jnp.stack([results["down"][1], results["up"][1]])[:, None]
    return (acts_out, ingrad_out, kvgrad_out)


def solution(mesh):
    in_specs = (
        P("seq", None),
        P("seq", None),
        P("seq", None),
        P("seq", None),
        P("section", None, None),
        P("section", None, None, None),
        P(),
    )
    out_specs = (
        P(None, "section", "seq", None),
        P(None, "section", "seq", None),
        P(None, "section", "seq", None),
    )
    return jax.shard_map(
        per_device, mesh=mesh, in_specs=in_specs, out_specs=out_specs, check_vma=False
    )
```

time: 493 us -> 403 us (0.82); the launches traced: 485 us -> 401 us
  Pallas kernels: 0 us -> 140 us
  starting transfers between devices: 154 us -> 69.9 us
  local copies, waits for them, and re-layouts: 73.1 us -> 6.26 us
  matrix products: 59.2 us -> 0 us
  other arithmetic: 68.2 us -> 32.5 us
  waiting for transfers between devices: 126 us -> 151 us
    pallas_call x0 -> x16, Pallas kernels: none -> 140 us  [the longest x4 48.9 us: reverse_mix(): pl.pallas_call(reverse_kernel, grid=(KV_HEADS,), in_specs=[block, block]...]
    ppermute x24, starting transfers between devices: 154 us -> 69.9 us  [passed_along(): return lax.ppermute(block, axis, route)]
    dot_general x18 -> x0, matrix products: 51 us -> none  [the longest x6 30.2 us: project_kv(): jnp.dot(normalize(stream, gain_row), weight_mat, preferred_element_type=j...]
    ppermute x24, waiting for transfers between devices: 126 us -> 151 us  [passed_along(): return lax.ppermute(block, axis, route)]
    cond x31 -> x0, local copies, waits for them, and re-layouts: 22.9 us -> none  [the longest x6 8.89 us: per_device(): lax.cond(active, reverse_mix, skip_mix, cotangent, layer_input, window)]
    squeeze x2 -> x0, local copies, waits for them, and re-layouts: 21.9 us -> none  [the longest x1 21.3 us: layer_setup(): lax.dynamic_index_in_dim(weight_pair, slot_index, 0, keepdims=False)]
    select_n x7 -> x15, other arithmetic: 7.49 us -> 24 us  [the longest x7 12.8 us: per_device(): jnp.where(down, a, b)]
    another operation x12 -> x1, local copies, waits for them, and re-layouts: 17 us -> 1.38 us  [per_device(): gain_pair = gains[0][:, None, :]]
  transfers between devices with their start and end apart: 24 -> 24, of which waited for: 19 -> 20; matrix products, arithmetic and copies ran while one was open for 11% -> 4% of each run, Pallas kernels for 0% -> 2%
where the time goes in v1:
time: 403 us; the launch traced here: 401 us
  waiting for transfers between devices  151 us (37%)
  Pallas kernels  140 us (35%)
  starting transfers between devices  69.9 us (17%)
  other arithmetic  32.5 us (8%)
  local copies, waits for them, and re-layouts  6.26 us (2%)
    ppermute x24, waiting for transfers between devices, passed_along(): return lax.ppermute(block, axis, route)  151 us
    ppermute x24, starting transfers between devices, passed_along(): return lax.ppermute(block, axis, route)  69.9 us
    pallas_call x4, Pallas kernels, reverse_mix(): pl.pallas_call(reverse_kernel, grid=(KV_HEADS,), in_specs=[block, block]...  48.9 us
    pallas_call x4, Pallas kernels, reverse_project(): pl.pallas_call(functools.partial(reverse_project_kernel, steps), grid_spe...  39.1 us
    pallas_call x4, Pallas kernels, mix(): pl.pallas_call(mix_kernel, grid=(KV_HEADS,), in_specs=[block, block] + he...  26.1 us
    pallas_call x4, Pallas kernels, project(): pl.pallas_call(project_kernel, grid_spec=pltpu.PrefetchScalarGridSpec(num...  26 us
    select_n x7, other arithmetic, per_device(): jnp.where(down, a, b)  12.8 us
  transfers between devices with their start and end apart: 24, of which 20 were waited for; matrix products, arithmetic and copies ran while one was open for 4% of the time, Pallas kernels for 2%

profile of v1, /device:TPU:27, one launch (start us, length us, event | category | flops | bytes accessed | tf_op | source)
XLA Modules:
  0.0 400.6 jit_solution(16161628530833109399)
XLA Ops:
  4.3 6.4 %project.4 = (bf16[128,1024]{1,0:T(8,128)(2,1)}, bf16[128,4096]{1,0:T(8,128)(2,1)}) custom-call(s32[1]{0:T(128)} %bitcast.slot_ref, bf16[128,4096]{1,0:T(8,128)(2,1)} %broadcast_select_fusion.3.h_ref, f32[2,1,4096]{2,1,0:T(1,128)} %broadcast_in_dim_squeeze.3.gain_ref, bf16[2,4096,1024]{2,1,0:T(8,128)(2,1)} %bitcast.33), custom_call_target="tpu_custom_call" | custom-call | flops 1073741824 | bytes 8388608 | tf_op jit(solution)/shard_map/project/pallas_call | solution.py:48
  18.8 6.5 %mix.4 = bf16[128,4096]{1,0:T(8,128)(2,1)} custom-call(bf16[128,4096]{1,0:T(8,128)(2,1)} %broadcast_select_fusion.3.h_ref, bf16[128,4096]{1,0:T(8,128)(2,1)} %get-tuple-element.39.normed_ref, bf16[128,1024]{1,0:T(8,128)(2,1)} %copy-done.18, bf16[128,1024]{1,0:T(8,128)(2,1)} %get-tuple-element.40.ko_ref.vo_ref, bf16[128,1024]{1,0:T(8,128)(2,1)} %copy-done.18, ...), custom_call_target="tpu_custom_call" | custom-call | flops 536870912 | bytes 3145728 | tf_op jit(solution)/shard_map/mix/pallas_call | solution.py:106
  30.6 20.2 %collective-permute-done.1 = bf16[128,4096]{1,0:T(8,128)(2,1)S(1)} collective-permute-done((bf16[128,4096]{1,0:T(8,128)(2,1)}, bf16[128,4096]{1,0:T(8,128)(2,1)S(1)}, u32[]{:S(2)}, u32[]{:S(2)}) %collective-permute-start.1) | collective-permute-done | bytes 1048608 | tf_op jit(solution)/shard_map/ppermute | solution.py:27
  52.8 6.5 %project.5 = (bf16[128,1024]{1,0:T(8,128)(2,1)}, bf16[128,4096]{1,0:T(8,128)(2,1)}) custom-call(s32[1]{0:T(128)} %bitcast.4.slot_ref, bf16[128,4096]{1,0:T(8,128)(2,1)} %broadcast_select_fusion.7.h_ref, f32[2,1,4096]{2,1,0:T(1,128)} %broadcast_in_dim_squeeze.3.gain_ref, bf16[2,4096,1024]{2,1,0:T(8,128)(2,1)} %bitcast.34), custom_call_target="tpu_custom_call" | custom-call | flops 1073741824 | bytes 8388608 | tf_op jit(solution)/shard_map/project/pallas_call | solution.py:48
  59.3 5.4 %collective-permute-start.3 = (bf16[128,1024]{1,0:T(8,128)(2,1)}, bf16[128,1024]{1,0:T(8,128)(2,1)S(1)}, u32[]{:S(2)}, u32[]{:S(2)}) collective-permute-start(bf16[128,1024]{1,0:T(8,128)(2,1)} %get-tuple-element.42.ko_ref.vo_ref), channel_id=1, source_target_pairs={{0,1},{1,2},{2,3},{3,4},{4,5},{5,6},{6,7},{8,9},{9,10},{10,11},{11... | collective-permute-start | bytes 786440 | tf_op jit(solution)/shard_map/ppermute | solution.py:27
  69.0 6.5 %mix.5 = bf16[128,4096]{1,0:T(8,128)(2,1)} custom-call(bf16[128,4096]{1,0:T(8,128)(2,1)} %broadcast_select_fusion.7.h_ref, bf16[128,4096]{1,0:T(8,128)(2,1)} %get-tuple-element.41.normed_ref, bf16[128,1024]{1,0:T(8,128)(2,1)} %copy-done.20, bf16[128,1024]{1,0:T(8,128)(2,1)} %get-tuple-element.42.ko_ref.vo_ref, bf16[128,1024]{1,0:T(8,128)(2,1)} %copy-done.20, ...), custom_call_target="tpu_custom_call" | custom-call | flops 536870912 | bytes 3145728 | tf_op jit(solution)/shard_map/mix/pallas_call | solution.py:106
  81.6 20.5 %collective-permute-done.4 = bf16[128,4096]{1,0:T(8,128)(2,1)S(1)} collective-permute-done((bf16[128,4096]{1,0:T(8,128)(2,1)}, bf16[128,4096]{1,0:T(8,128)(2,1)S(1)}, u32[]{:S(2)}, u32[]{:S(2)}) %collective-permute-start.4) | collective-permute-done | bytes 1048608 | tf_op jit(solution)/shard_map/ppermute | solution.py:27
  104.1 6.5 %project.6 = (bf16[128,1024]{1,0:T(8,128)(2,1)}, bf16[128,4096]{1,0:T(8,128)(2,1)}) custom-call(s32[1]{0:T(128)} %bitcast.5.slot_ref, bf16[128,4096]{1,0:T(8,128)(2,1)} %broadcast_select_fusion.11.h_ref, f32[2,1,4096]{2,1,0:T(1,128)} %broadcast_in_dim_squeeze.3.gain_ref, bf16[2,4096,1024]{2,1,0:T(8,128)(2,1)} %bitcast.35), custom_call_target="tpu_custom_call" | custom-call | flops 1073741824 | bytes 8388608 | tf_op jit(solution)/shard_map/project/pallas_call | solution.py:48
  116.8 6.5 %mix.6 = bf16[128,4096]{1,0:T(8,128)(2,1)} custom-call(bf16[128,4096]{1,0:T(8,128)(2,1)} %broadcast_select_fusion.11.h_ref, bf16[128,4096]{1,0:T(8,128)(2,1)} %get-tuple-element.43.normed_ref, bf16[128,1024]{1,0:T(8,128)(2,1)} %copy-done.22, bf16[128,1024]{1,0:T(8,128)(2,1)} %get-tuple-element.44.ko_ref.vo_ref, bf16[128,1024]{1,0:T(8,128)(2,1)} %copy-done.22, ...), custom_call_target="tpu_custom_call" | custom-call | flops 536870912 | bytes 3145728 | tf_op jit(solution)/shard_map/mix/pallas_call | solution.py:106
  124.9 5.6 %collective-permute-start.8 = (bf16[128,4096]{1,0:T(8,128)(2,1)}, bf16[128,4096]{1,0:T(8,128)(2,1)}, u32[]{:S(2)}, u32[]{:S(2)}) collective-permute-start(bf16[128,4096]{1,0:T(8,128)(2,1)} %mix.6), channel_id=1, source_target_pairs={{8,0},{16,8},{24,16},{9,1},{17,9},{25,17},{10,2},{18,10},{26,18},{... | collective-permute-start | bytes 3145736 | tf_op jit(solution)/shard_map/ppermute | solution.py:27
  133.0 14.0 %collective-permute-done.7 = bf16[128,4096]{1,0:T(8,128)(2,1)} collective-permute-done((bf16[128,4096]{1,0:T(8,128)(2,1)}, bf16[128,4096]{1,0:T(8,128)(2,1)}, u32[]{:S(2)}, u32[]{:S(2)}) %collective-permute-start.7) | collective-permute-done | bytes 1048608 | tf_op jit(solution)/shard_map/ppermute | solution.py:27
  151.6 6.6 %project.7 = (bf16[128,1024]{1,0:T(8,128)(2,1)}, bf16[128,4096]{1,0:T(8,128)(2,1)}) custom-call(s32[1]{0:T(128)} %bitcast.6.slot_ref, bf16[128,4096]{1,0:T(8,128)(2,1)} %get-tuple-element.88.h_ref, f32[2,1,4096]{2,1,0:T(1,128)} %broadcast_in_dim_squeeze.3.gain_ref, bf16[2,4096,1024]{2,1,0:T(8,128)(2,1)} %bitcast.36), custom_call_target="tpu_custom_call" | custom-call | flops 1073741824 | bytes 8388608 | tf_op jit(solution)/shard_map/project/pallas_call | solution.py:48
  170.4 12.3 %reverse_mix.4 = (bf16[128,4096]{1,0:T(8,128)(2,1)}, bf16[128,512]{1,0:T(8,128)(2,1)}, bf16[128,512]{1,0:T(8,128)(2,1)}, bf16[128,512]{1,0:T(8,128)(2,1)}, bf16[128,512]{1,0:T(8,128)(2,1)}) custom-call(bf16[128,4096]{1,0:T(8,128)(2,1)} %broadcast_select_fusion.14.c_ref, bf16[128,4096]{1,0:T(8,128)(2,1)} %get-tuple-element.107.normed_ref, ...), custom_call_target="tpu_custom_call" | custom-call | flops 1342177280 | bytes 3145728 | tf_op jit(solution)/shard_map/reverse_mix/pallas_call | solution.py:158
  195.8 9.7 %reverse_project.4 = (bf16[128,4096]{1,0:T(8,128)(2,1)}, bf16[128,1024]{1,0:T(8,128)(2,1)}) custom-call(s32[1]{0:T(128)} %bitcast.6.slot_ref, bf16[128,4096]{1,0:T(8,128)(2,1)} %broadcast_select_fusion.14.c_ref, bf16[128,4096]{1,0:T(8,128)(2,1)} %get-tuple-element.47.dq_ref, bf16[128,4096]{1,0:T(8,128)(2,1)} %get-tuple-element.104.h_ref, ...), custom_call_target="tpu_custom_call" | custom-call | flops 1073741824 | bytes 8388608 | tf_op jit(solution)/shard_map/reverse_project/pallas_call | solution.py:211
  211.0 20.9 %collective-permute-done.12 = bf16[128,4096]{1,0:T(8,128)(2,1)S(1)} collective-permute-done((bf16[128,4096]{1,0:T(8,128)(2,1)}, bf16[128,4096]{1,0:T(8,128)(2,1)S(1)}, u32[]{:S(2)}, u32[]{:S(2)}) %collective-permute-start.12) | collective-permute-done | bytes 1048608 | tf_op jit(solution)/shard_map/ppermute | solution.py:27
  237.2 12.2 %reverse_mix.5 = (bf16[128,4096]{1,0:T(8,128)(2,1)}, bf16[128,512]{1,0:T(8,128)(2,1)}, bf16[128,512]{1,0:T(8,128)(2,1)}, bf16[128,512]{1,0:T(8,128)(2,1)}, bf16[128,512]{1,0:T(8,128)(2,1)}) custom-call(bf16[128,4096]{1,0:T(8,128)(2,1)} %broadcast_select_fusion.10.c_ref, bf16[128,4096]{1,0:T(8,128)(2,1)} %get-tuple-element.106.normed_ref, ...), custom_call_target="tpu_custom_call" | custom-call | flops 1342177280 | bytes 3145728 | tf_op jit(solution)/shard_map/reverse_mix/pallas_call | solution.py:158
  259.3 9.8 %reverse_project.5 = (bf16[128,4096]{1,0:T(8,128)(2,1)}, bf16[128,1024]{1,0:T(8,128)(2,1)}) custom-call(s32[1]{0:T(128)} %bitcast.5.slot_ref, bf16[128,4096]{1,0:T(8,128)(2,1)} %broadcast_select_fusion.10.c_ref, bf16[128,4096]{1,0:T(8,128)(2,1)} %get-tuple-element.53.dq_ref, bf16[128,4096]{1,0:T(8,128)(2,1)} %get-tuple-element.103.h_ref, ...), custom_call_target="tpu_custom_call" | custom-call | flops 1073741824 | bytes 8388608 | tf_op jit(solution)/shard_map/reverse_project/pallas_call | solution.py:211
  274.4 19.2 %collective-permute-done.16 = bf16[128,4096]{1,0:T(8,128)(2,1)S(1)} collective-permute-done((bf16[128,4096]{1,0:T(8,128)(2,1)}, bf16[128,4096]{1,0:T(8,128)(2,1)S(1)}, u32[]{:S(2)}, u32[]{:S(2)}) %collective-permute-start.16) | collective-permute-done | bytes 1048608 | tf_op jit(solution)/shard_map/ppermute | solution.py:27
  299.0 12.2 %reverse_mix.6 = (bf16[128,4096]{1,0:T(8,128)(2,1)}, bf16[128,512]{1,0:T(8,128)(2,1)}, bf16[128,512]{1,0:T(8,128)(2,1)}, bf16[128,512]{1,0:T(8,128)(2,1)}, bf16[128,512]{1,0:T(8,128)(2,1)}) custom-call(bf16[128,4096]{1,0:T(8,128)(2,1)} %broadcast_select_fusion.6.c_ref, bf16[128,4096]{1,0:T(8,128)(2,1)} %get-tuple-element.105.normed_ref, ...), custom_call_target="tpu_custom_call" | custom-call | flops 1342177280 | bytes 3145728 | tf_op jit(solution)/shard_map/reverse_mix/pallas_call | solution.py:158
  315.0 6.5 %mix.7 = bf16[128,4096]{1,0:T(8,128)(2,1)} custom-call(bf16[128,4096]{1,0:T(8,128)(2,1)} %get-tuple-element.88.h_ref, bf16[128,4096]{1,0:T(8,128)(2,1)} %get-tuple-element.45.normed_ref, bf16[128,1024]{1,0:T(8,128)(2,1)} %copy-done.17, bf16[128,1024]{1,0:T(8,128)(2,1)} %get-tuple-element.46.ko_ref.vo_ref, bf16[128,1024]{1,0:T(8,128)(2,1)} %copy-done.17, ...), custom_call_target="tpu_custom_call" | custom-call | flops 536870912 | bytes 3145728 | tf_op jit(solution)/shard_map/mix/pallas_call | solution.py:106
  322.3 9.8 %reverse_project.6 = (bf16[128,4096]{1,0:T(8,128)(2,1)}, bf16[128,1024]{1,0:T(8,128)(2,1)}) custom-call(s32[1]{0:T(128)} %bitcast.4.slot_ref, bf16[128,4096]{1,0:T(8,128)(2,1)} %broadcast_select_fusion.6.c_ref, bf16[128,4096]{1,0:T(8,128)(2,1)} %get-tuple-element.59.dq_ref, bf16[128,4096]{1,0:T(8,128)(2,1)} %get-tuple-element.102.h_ref, ...), custom_call_target="tpu_custom_call" | custom-call | flops 1073741824 | bytes 8388608 | tf_op jit(solution)/shard_map/reverse_project/pallas_call | solution.py:211
  339.9 18.3 %collective-permute-done.20 = bf16[128,4096]{1,0:T(8,128)(2,1)S(1)} collective-permute-done((bf16[128,4096]{1,0:T(8,128)(2,1)}, bf16[128,4096]{1,0:T(8,128)(2,1)S(1)}, u32[]{:S(2)}, u32[]{:S(2)}) %collective-permute-start.20) | collective-permute-done | bytes 1048608 | tf_op jit(solution)/shard_map/ppermute | solution.py:27
  363.4 12.3 %reverse_mix.7 = (bf16[128,4096]{1,0:T(8,128)(2,1)}, bf16[128,512]{1,0:T(8,128)(2,1)}, bf16[128,512]{1,0:T(8,128)(2,1)}, bf16[128,512]{1,0:T(8,128)(2,1)}, bf16[128,512]{1,0:T(8,128)(2,1)}) custom-call(bf16[128,4096]{1,0:T(8,128)(2,1)} %broadcast_select_fusion.2.c_ref, bf16[128,4096]{1,0:T(8,128)(2,1)} %get-tuple-element.95.normed_ref, ...), custom_call_target="tpu_custom_call" | custom-call | flops 1342177280 | bytes 3145728 | tf_op jit(solution)/shard_map/reverse_mix/pallas_call | solution.py:158
  386.8 9.8 %reverse_project.7 = (bf16[128,4096]{1,0:T(8,128)(2,1)}, bf16[128,1024]{1,0:T(8,128)(2,1)}) custom-call(s32[1]{0:T(128)} %bitcast.slot_ref, bf16[128,4096]{1,0:T(8,128)(2,1)} %broadcast_select_fusion.2.c_ref, bf16[128,4096]{1,0:T(8,128)(2,1)} %get-tuple-element.65.dq_ref, bf16[128,4096]{1,0:T(8,128)(2,1)} %get-tuple-element.85.h_ref, ...), custom_call_target="tpu_custom_call" | custom-call | flops 1073741824 | bytes 8388608 | tf_op jit(solution)/shard_map/reverse_project/pallas_call | solution.py:211
  (149 shorter events, 135.2 us)
Async XLA Ops:
  10.8 7.3 %collective-permute-start = (bf16[128,1024]{1,0:T(8,128)(2,1)}, bf16[128,1024]{1,0:T(8,128)(2,1)S(1)}, u32[]{:S(2)}, u32[]{:S(2)}) collective-permute-start(bf16[128,1024]{1,0:T(8,128)(2,1)} %get-tuple-element.40.ko_ref.vo_ref), channel_id=1, source_target_pairs={{0,1},{1,2},{2,3},{3,4},{4,5},{5,6},{6,7},{8,9},{9,10},{10,11},{11... | collective-permute-start | bytes 786440 | tf_op jit(solution)/shard_map/ppermute | solution.py:27
  25.3 25.5 %collective-permute-start.1 = (bf16[128,4096]{1,0:T(8,128)(2,1)}, bf16[128,4096]{1,0:T(8,128)(2,1)S(1)}, u32[]{:S(2)}, u32[]{:S(2)}) collective-permute-start(bf16[128,4096]{1,0:T(8,128)(2,1)} %mix.4), channel_id=1, source_target_pairs={{0,8},{8,16},{16,24},{1,9},{9,17},{17,25},{2,10},{10,18},{18,26},{... | collective-permute-start | bytes 3145736 | tf_op jit(solution)/shard_map/ppermute | solution.py:27
  26.5 25.2 %collective-permute-start.2 = (bf16[128,4096]{1,0:T(8,128)(2,1)}, bf16[128,4096]{1,0:T(8,128)(2,1)S(1)}, u32[]{:S(2)}, u32[]{:S(2)}) collective-permute-start(bf16[128,4096]{1,0:T(8,128)(2,1)} %mix.4), channel_id=1, source_target_pairs={{8,0},{16,8},{24,16},{9,1},{17,9},{25,17},{10,2},{18,10},{26,18},{... | collective-permute-start | bytes 3145736 | tf_op jit(solution)/shard_map/ppermute | solution.py:27
  59.3 9.0 %collective-permute-start.3 = (bf16[128,1024]{1,0:T(8,128)(2,1)}, bf16[128,1024]{1,0:T(8,128)(2,1)S(1)}, u32[]{:S(2)}, u32[]{:S(2)}) collective-permute-start(bf16[128,1024]{1,0:T(8,128)(2,1)} %get-tuple-element.42.ko_ref.vo_ref), channel_id=1, source_target_pairs={{0,1},{1,2},{2,3},{3,4},{4,5},{5,6},{6,7},{8,9},{9,10},{10,11},{11... | collective-permute-start | bytes 786440 | tf_op jit(solution)/shard_map/ppermute | solution.py:27
  75.6 26.4 %collective-permute-start.4 = (bf16[128,4096]{1,0:T(8,128)(2,1)}, bf16[128,4096]{1,0:T(8,128)(2,1)S(1)}, u32[]{:S(2)}, u32[]{:S(2)}) collective-permute-start(bf16[128,4096]{1,0:T(8,128)(2,1)} %mix.5), channel_id=1, source_target_pairs={{0,8},{8,16},{16,24},{1,9},{9,17},{17,25},{2,10},{10,18},{18,26},{... | collective-permute-start | bytes 3145736 | tf_op jit(solution)/shard_map/ppermute | solution.py:27
  76.9 26.2 %collective-permute-start.5 = (bf16[128,4096]{1,0:T(8,128)(2,1)}, bf16[128,4096]{1,0:T(8,128)(2,1)S(1)}, u32[]{:S(2)}, u32[]{:S(2)}) collective-permute-start(bf16[128,4096]{1,0:T(8,128)(2,1)} %mix.5), channel_id=1, source_target_pairs={{8,0},{16,8},{24,16},{9,1},{17,9},{25,17},{10,2},{18,10},{26,18},{... | collective-permute-start | bytes 3145736 | tf_op jit(solution)/shard_map/ppermute | solution.py:27
  110.6 5.5 %collective-permute-start.6 = (bf16[128,1024]{1,0:T(8,128)(2,1)}, bf16[128,1024]{1,0:T(8,128)(2,1)S(1)}, u32[]{:S(2)}, u32[]{:S(2)}) collective-permute-start(bf16[128,1024]{1,0:T(8,128)(2,1)} %get-tuple-element.44.ko_ref.vo_ref), channel_id=1, source_target_pairs={{0,1},{1,2},{2,3},{3,4},{4,5},{5,6},{6,7},{8,9},{9,10},{10,11},{11... | collective-permute-start | bytes 786440 | tf_op jit(solution)/shard_map/ppermute | solution.py:27
  123.4 23.6 %collective-permute-start.7 = (bf16[128,4096]{1,0:T(8,128)(2,1)}, bf16[128,4096]{1,0:T(8,128)(2,1)}, u32[]{:S(2)}, u32[]{:S(2)}) collective-permute-start(bf16[128,4096]{1,0:T(8,128)(2,1)} %mix.6), channel_id=1, source_target_pairs={{0,8},{8,16},{16,24},{1,9},{9,17},{17,25},{2,10},{10,18},{18,26},{... | collective-permute-start | bytes 3145736 | tf_op jit(solution)/shard_map/ppermute | solution.py:27
  124.9 22.9 %collective-permute-start.8 = (bf16[128,4096]{1,0:T(8,128)(2,1)}, bf16[128,4096]{1,0:T(8,128)(2,1)}, u32[]{:S(2)}, u32[]{:S(2)}) collective-permute-start(bf16[128,4096]{1,0:T(8,128)(2,1)} %mix.6), channel_id=1, source_target_pairs={{8,0},{16,8},{24,16},{9,1},{17,9},{25,17},{10,2},{18,10},{26,18},{... | collective-permute-start | bytes 3145736 | tf_op jit(solution)/shard_map/ppermute | solution.py:27
  158.3 10.1 %collective-permute-start.9 = (bf16[128,1024]{1,0:T(8,128)(2,1)}, bf16[128,1024]{1,0:T(8,128)(2,1)S(1)}, u32[]{:S(2)}, u32[]{:S(2)}) collective-permute-start(bf16[128,1024]{1,0:T(8,128)(2,1)} %get-tuple-element.46.ko_ref.vo_ref), channel_id=1, source_target_pairs={{0,1},{1,2},{2,3},{3,4},{4,5},{5,6},{6,7},{8,9},{9,10},{10,11},{11... | collective-permute-start | bytes 786440 | tf_op jit(solution)/shard_map/ppermute | solution.py:27
  182.7 10.1 %collective-permute-start.10 = (bf16[128,512]{1,0:T(8,128)(2,1)}, bf16[128,512]{1,0:T(8,128)(2,1)S(1)}, u32[]{:S(2)}, u32[]{:S(2)}) collective-permute-start(bf16[128,512]{1,0:T(8,128)(2,1)} %get-tuple-element.49), channel_id=1, source_target_pairs={{1,0},{2,1},{3,2},{4,3},{5,4},{6,5},{7,6},{9,8},{10,9},{11,10},{12... | collective-permute-start | bytes 393224 | tf_op jit(solution)/shard_map/ppermute | solution.py:27
  187.8 7.4 %collective-permute-start.11 = (bf16[128,512]{1,0:T(8,128)(2,1)}, bf16[128,512]{1,0:T(8,128)(2,1)S(1)}, u32[]{:S(2)}, u32[]{:S(2)}) collective-permute-start(bf16[128,512]{1,0:T(8,128)(2,1)} %get-tuple-element.51), channel_id=1, source_target_pairs={{1,0},{2,1},{3,2},{4,3},{5,4},{6,5},{7,6},{9,8},{10,9},{11,10},{12... | collective-permute-start | bytes 393224 | tf_op jit(solution)/shard_map/ppermute | solution.py:27
  205.6 26.4 %collective-permute-start.12 = (bf16[128,4096]{1,0:T(8,128)(2,1)}, bf16[128,4096]{1,0:T(8,128)(2,1)S(1)}, u32[]{:S(2)}, u32[]{:S(2)}) collective-permute-start(bf16[128,4096]{1,0:T(8,128)(2,1)} %get-tuple-element.52), channel_id=1, source_target_pairs={{8,0},{16,8},{24,16},{9,1},{17,9},{25,17},{10,2},{18,10},{26,18},{... | collective-permute-start | bytes 3145736 | tf_op jit(solution)/shard_map/ppermute | solution.py:27
  209.7 26.3 %collective-permute-start.13 = (bf16[128,4096]{1,0:T(8,128)(2,1)}, bf16[128,4096]{1,0:T(8,128)(2,1)S(1)}, u32[]{:S(2)}, u32[]{:S(2)}) collective-permute-start(bf16[128,4096]{1,0:T(8,128)(2,1)} %get-tuple-element.52), channel_id=1, source_target_pairs={{0,8},{8,16},{16,24},{1,9},{9,17},{17,25},{2,10},{10,18},{18,26},{... | collective-permute-start | bytes 3145736 | tf_op jit(solution)/shard_map/ppermute | solution.py:27
  249.3 7.4 %collective-permute-start.14 = (bf16[128,512]{1,0:T(8,128)(2,1)}, bf16[128,512]{1,0:T(8,128)(2,1)S(1)}, u32[]{:S(2)}, u32[]{:S(2)}) collective-permute-start(bf16[128,512]{1,0:T(8,128)(2,1)} %get-tuple-element.55), channel_id=1, source_target_pairs={{1,0},{2,1},{3,2},{4,3},{5,4},{6,5},{7,6},{9,8},{10,9},{11,10},{12... | collective-permute-start | bytes 393224 | tf_op jit(solution)/shard_map/ppermute | solution.py:27
  251.3 7.4 %collective-permute-start.15 = (bf16[128,512]{1,0:T(8,128)(2,1)}, bf16[128,512]{1,0:T(8,128)(2,1)S(1)}, u32[]{:S(2)}, u32[]{:S(2)}) collective-permute-start(bf16[128,512]{1,0:T(8,128)(2,1)} %get-tuple-element.57), channel_id=1, source_target_pairs={{1,0},{2,1},{3,2},{4,3},{5,4},{6,5},{7,6},{9,8},{10,9},{11,10},{12... | collective-permute-start | bytes 393224 | tf_op jit(solution)/shard_map/ppermute | solution.py:27
  269.1 24.5 %collective-permute-start.16 = (bf16[128,4096]{1,0:T(8,128)(2,1)}, bf16[128,4096]{1,0:T(8,128)(2,1)S(1)}, u32[]{:S(2)}, u32[]{:S(2)}) collective-permute-start(bf16[128,4096]{1,0:T(8,128)(2,1)} %get-tuple-element.58), channel_id=1, source_target_pairs={{8,0},{16,8},{24,16},{9,1},{17,9},{25,17},{10,2},{18,10},{26,18},{... | collective-permute-start | bytes 3145736 | tf_op jit(solution)/shard_map/ppermute | solution.py:27
  272.9 25.0 %collective-permute-start.17 = (bf16[128,4096]{1,0:T(8,128)(2,1)}, bf16[128,4096]{1,0:T(8,128)(2,1)S(1)}, u32[]{:S(2)}, u32[]{:S(2)}) collective-permute-start(bf16[128,4096]{1,0:T(8,128)(2,1)} %get-tuple-element.58), channel_id=1, source_target_pairs={{0,8},{8,16},{16,24},{1,9},{9,17},{17,25},{2,10},{10,18},{18,26},{... | collective-permute-start | bytes 3145736 | tf_op jit(solution)/shard_map/ppermute | solution.py:27
  311.2 10.4 %collective-permute-start.18 = (bf16[128,512]{1,0:T(8,128)(2,1)}, bf16[128,512]{1,0:T(8,128)(2,1)S(1)}, u32[]{:S(2)}, u32[]{:S(2)}) collective-permute-start(bf16[128,512]{1,0:T(8,128)(2,1)} %get-tuple-element.61), channel_id=1, source_target_pairs={{1,0},{2,1},{3,2},{4,3},{5,4},{6,5},{7,6},{9,8},{10,9},{11,10},{12... | collective-permute-start | bytes 393224 | tf_op jit(solution)/shard_map/ppermute | solution.py:27
  313.1 8.5 %collective-permute-start.19 = (bf16[128,512]{1,0:T(8,128)(2,1)}, bf16[128,512]{1,0:T(8,128)(2,1)S(1)}, u32[]{:S(2)}, u32[]{:S(2)}) collective-permute-start(bf16[128,512]{1,0:T(8,128)(2,1)} %get-tuple-element.63), channel_id=1, source_target_pairs={{1,0},{2,1},{3,2},{4,3},{5,4},{6,5},{7,6},{9,8},{10,9},{11,10},{12... | collective-permute-start | bytes 393224 | tf_op jit(solution)/shard_map/ppermute | solution.py:27
  332.1 26.1 %collective-permute-start.20 = (bf16[128,4096]{1,0:T(8,128)(2,1)}, bf16[128,4096]{1,0:T(8,128)(2,1)S(1)}, u32[]{:S(2)}, u32[]{:S(2)}) collective-permute-start(bf16[128,4096]{1,0:T(8,128)(2,1)} %get-tuple-element.64), channel_id=1, source_target_pairs={{8,0},{16,8},{24,16},{9,1},{17,9},{25,17},{10,2},{18,10},{26,18},{... | collective-permute-start | bytes 3145736 | tf_op jit(solution)/shard_map/ppermute | solution.py:27
  335.8 26.5 %collective-permute-start.21 = (bf16[128,4096]{1,0:T(8,128)(2,1)}, bf16[128,4096]{1,0:T(8,128)(2,1)S(1)}, u32[]{:S(2)}, u32[]{:S(2)}) collective-permute-start(bf16[128,4096]{1,0:T(8,128)(2,1)} %get-tuple-element.64), channel_id=1, source_target_pairs={{0,8},{8,16},{16,24},{1,9},{9,17},{17,25},{2,10},{10,18},{18,26},{... | collective-permute-start | bytes 3145736 | tf_op jit(solution)/shard_map/ppermute | solution.py:27
  375.7 8.6 %collective-permute-start.22 = (bf16[128,512]{1,0:T(8,128)(2,1)}, bf16[128,512]{1,0:T(8,128)(2,1)S(1)}, u32[]{:S(2)}, u32[]{:S(2)}) collective-permute-start(bf16[128,512]{1,0:T(8,128)(2,1)} %get-tuple-element.67), channel_id=1, source_target_pairs={{1,0},{2,1},{3,2},{4,3},{5,4},{6,5},{7,6},{9,8},{10,9},{11,10},{12... | collective-permute-start | bytes 393224 | tf_op jit(solution)/shard_map/ppermute | solution.py:27
  377.8 8.4 %collective-permute-start.23 = (bf16[128,512]{1,0:T(8,128)(2,1)}, bf16[128,512]{1,0:T(8,128)(2,1)S(1)}, u32[]{:S(2)}, u32[]{:S(2)}) collective-permute-start(bf16[128,512]{1,0:T(8,128)(2,1)} %get-tuple-element.69), channel_id=1, source_target_pairs={{1,0},{2,1},{3,2},{4,3},{5,4},{6,5},{7,6},{9,8},{10,9},{11,10},{12... | collective-permute-start | bytes 393224 | tf_op jit(solution)/shard_map/ppermute | solution.py:27
  (40 other events, 301.8 us)
